TPU v7x, 32 devices: a whole 2x2x4 slice. The times are simulated.
32 devices in a mesh: seq: 8 (over z, y), head: 4 (over x, core).
Axes of the slice: x: 2, y: 2, z: 4, core: 2. Of those that a mesh axis runs over, the one named last changes fastest.
Arguments:
- tokens: bfloat16 [2048, 1024], P('seq'), may hold values from -6 to 6
- w_qkv: bfloat16 [1024, 3, 1024], P('seq', None, 'head'), may hold values from -0.1875 to 0.1875
- w_out: bfloat16 [1024, 1024], P('head', 'seq'), may hold values from -1 to 1
- ln1_gain: bfloat16 [1024], P('seq'), may hold values from 0.5 to 1.5
- ln1_bias: bfloat16 [1024], P('seq'), may hold values from -1.796875 to 1.796875
- ln2_gain: bfloat16 [1024], P('seq'), may hold values from 0.5 to 1.5
- ln2_bias: bfloat16 [1024], P('seq'), may hold values from -1.796875 to 1.796875
- w_up: bfloat16 [1024, 4096], P('seq', 'head'), may hold values from -0.1875 to 0.1875
- up_bias: bfloat16 [4096], P('head'), may hold values from -1.796875 to 1.796875
- w_down: bfloat16 [4096, 1024], P('head', 'seq'), may hold values from -0.09375 to 0.09375
- down_bias: bfloat16 [1024], P('seq'), may hold values from -1.796875 to 1.796875
- seq_units: int32 [4], replicated, may hold values from 1 to 4, 8 in all
- seq_pad: int32 [4], replicated, may hold values from 0 to 127
- rand_picks: int32 [32, 16, 3], P('seq', 'head'), may hold values from 0 to 65535
- cotangent: bfloat16 [2048, 1024], P('seq'), may hold values from -6 to 6
Outputs:
- output: bfloat16 [2048, 1024], P('seq')
- x_grad: float32 [2048, 1024], P('seq')
- w_qkv_grad: float32 [1024, 3, 1024], P('seq', None, 'head')
- w_out_grad: float32 [1024, 1024], P('head', 'seq')
- ln1_gain_grad: float32 [1024], P('seq')
- ln1_bias_grad: float32 [1024], P('seq')
- ln2_gain_grad: float32 [1024], P('seq')
- ln2_bias_grad: float32 [1024], P('seq')
- w_up_grad: float32 [1024, 4096], P('seq', 'head')
- up_bias_grad: float32 [4096], P('head')
- w_down_grad: float32 [4096, 1024], P('head', 'seq')
- down_bias_grad: float32 [1024], P('seq')
Inputs may be any that keep to these rules, and one draw needn't show every extreme that they name: `seq_units`: each sequence covers whole units; the values add up to the number of units in the stream, and some sequence covers 4 units.
All inputs are finite; a program needn't handle non-finite values.
Results may differ from a plain program's by a relative error of at most 0.012.
Values may be sent and summed in bfloat16 or wider, within the bound.
A program may use at most 128 MiB of HBM per device.

v0:
```python
import jax
import jax.numpy as jnp
from jax import lax
from jax.sharding import PartitionSpec as P

HEAD_DIM = 64
BLK = 64
SPAN = 4
BLK_DEV = 4
EPSILON = 1e-05
NEGATIVE = -1e30
F32 = jnp.float32
BF16 = jnp.bfloat16


def shifted(value, axis, steps):
    count = lax.axis_size(axis)
    first, last = (max(0, -steps), min(count, count - steps))
    return lax.ppermute(value, axis, [(i, i + steps) for i in range(first, last)])


def norm_parts(features):
    average = jnp.mean(features, axis=-1, keepdims=True)
    centred = features - average
    spread = jnp.mean(centred * centred, axis=-1, keepdims=True)
    inverse = lax.rsqrt(spread + EPSILON)
    return (centred * inverse, inverse)


def norm_backward(xhat, inverse, scaled):
    first = jnp.mean(scaled, axis=-1, keepdims=True)
    second = jnp.mean(scaled * xhat, axis=-1, keepdims=True)
    return inverse * (scaled - first - xhat * second)


def dot(a, b, dims):
    return lax.dot_general(a, b, (dims, ((), ())), preferred_element_type=F32)


def sequence_place(seq_units, seq_pad):
    device = lax.axis_index("seq")
    start, leader, span, pad = (0, 0, 0, 0)
    for k in range(seq_units.shape[0]):
        units = seq_units[k]
        inside = (device >= start) & (device < start + units)
        leader = jnp.where(inside, start, leader)
        span = jnp.where(inside, units, span)
        pad = jnp.where(inside, seq_pad[k], pad)
        start = start + units
    return (device - leader, span, pad)


def key_counts(position, span, picks):
    blocks = lax.broadcasted_iota(jnp.int32, (1, 1, SPAN * BLK_DEV), 2)
    query = position * BLK_DEV + lax.broadcasted_iota(jnp.int32, (BLK_DEV, 1, 1), 0)
    total = span * BLK_DEV
    count = jnp.zeros((BLK_DEV, picks.shape[1], SPAN * BLK_DEV), F32)
    for wanted in (query - 1, query, query + 1, 0, total - 1):
        count = count + (blocks == wanted).astype(F32)
    chosen = picks % total
    for r in range(picks.shape[2]):
        count = count + (blocks == chosen[:, :, r : r + 1]).astype(F32)
    return jnp.where((query == 0) | (query == total - 1), 1.0, count)


def local_general(
    tokens,
    w_qkv,
    w_out,
    ln1_gain,
    ln1_bias,
    ln2_gain,
    ln2_bias,
    w_up,
    up_bias,
    w_down,
    down_bias,
    seq_units,
    seq_pad,
    rand_picks,
    cotangent,
):
    tok, width = tokens.shape
    heads = w_qkv.shape[2] // HEAD_DIM
    rows = lambda v: lax.all_gather(v, "seq", axis=0, tiled=True)
    cols = lambda v: lax.all_gather(v, "seq", axis=1, tiled=True)
    vectors = jnp.stack([ln1_gain, ln1_bias, ln2_gain, ln2_bias, down_bias], axis=0)
    gain_one, shift_one, gain_two, shift_two, down_shift = [
        v[None].astype(F32) for v in cols(vectors)
    ]
    qkv = rows(w_qkv)
    out_w, up_w, down_w = (cols(w_out), rows(w_up), cols(w_down))
    position, span, pad = sequence_place(seq_units, seq_pad)
    root = SPAN - 1 - position
    inputs = tokens.astype(F32)
    xhat_one, inv_one = norm_parts(inputs)
    normed = (xhat_one * gain_one + shift_one).astype(BF16)
    triple = jnp.einsum("td,dcf->tcf", normed, qkv, preferred_element_type=F32).astype(BF16)
    own = jnp.stack([triple[:, 1], triple[:, 2]], axis=0)
    pieces = [own if o == 0 else shifted(own, "seq", -o) for o in range(1 - SPAN, SPAN)]
    nearby = jnp.stack(pieces, axis=0)
    window = lax.dynamic_slice_in_dim(nearby, root, SPAN, 0)
    split = lambda v: v.reshape(v.shape[0], heads, HEAD_DIM)
    keys = split(window[:, 0].reshape(SPAN * tok, -1))
    values = split(window[:, 1].reshape(SPAN * tok, -1))
    queries = split(triple[:, 0])
    scaling = HEAD_DIM ** (-0.5)
    live = jnp.arange(SPAN * tok, dtype=jnp.int32) < span * tok - pad
    count = jnp.repeat(key_counts(position, span, rand_picks), BLK, axis=2)
    count = jnp.where(live[None, None], count, 0.0)
    count = jnp.transpose(jnp.repeat(count, BLK, axis=0), (1, 0, 2))
    logits = jnp.einsum("qhd,khd->hqk", queries, keys, preferred_element_type=F32) * scaling
    logits = jnp.where(count > 0, logits, NEGATIVE)
    grown = jnp.exp(logits - jnp.max(logits, axis=-1, keepdims=True)) * count
    chances = grown / jnp.sum(grown, axis=-1, keepdims=True)
    chances_low = chances.astype(BF16)
    attended = jnp.einsum("hqk,khd->qhd", chances_low, values, preferred_element_type=F32)
    attended = attended.astype(BF16).reshape(tok, heads * HEAD_DIM)
    middle = inputs + lax.psum(dot(attended, out_w, ((1,), (0,))), "head")
    xhat_two, inv_two = norm_parts(middle)
    normed_two = (xhat_two * gain_two + shift_two).astype(BF16)
    pre_act = dot(normed_two, up_w, ((1,), (0,))) + up_bias.astype(F32)[None]
    hidden, pull = jax.vjp(lambda v: jax.nn.gelu(v, approximate=True), pre_act)
    hidden = hidden.astype(BF16)
    ffn = lax.psum(dot(hidden, down_w, ((1,), (0,))).astype(BF16), "head").astype(F32)
    output = (middle + ffn + down_shift).astype(BF16)
    grad_out = cotangent.astype(F32)
    grad_w_down = dot(hidden, cotangent, ((0,), (0,)))
    grad_pre = pull(dot(cotangent, down_w, ((1,), (1,))))[0].astype(BF16)
    grad_w_up = dot(normed_two, grad_pre, ((0,), (0,)))
    grad_up_bias = lax.psum(jnp.sum(grad_pre.astype(F32), axis=0), "seq")
    grad_two = lax.psum(dot(grad_pre, up_w, ((1,), (1,))), "head")
    grad_middle = grad_out + norm_backward(xhat_two, inv_two, grad_two * gain_two)
    grad_branch = grad_middle.astype(BF16)
    grad_w_out = dot(attended, grad_branch, ((0,), (0,)))
    grad_att = split(dot(grad_branch, out_w, ((1,), (1,))).astype(BF16))
    grad_prob = jnp.einsum("qhd,khd->hqk", grad_att, values, preferred_element_type=F32)
    inner = jnp.sum(chances * grad_prob, axis=-1, keepdims=True)
    grad_logit = (chances * (grad_prob - inner)).astype(BF16)
    dq = scaling * jnp.einsum("hqk,khd->qhd", grad_logit, keys, preferred_element_type=F32)
    dk = scaling * jnp.einsum("hqk,qhd->khd", grad_logit, queries, preferred_element_type=F32)
    dv = jnp.einsum("hqk,qhd->khd", chances_low, grad_att, preferred_element_type=F32)
    part = jnp.stack([dk.reshape(SPAN, tok, -1), dv.reshape(SPAN, tok, -1)], axis=1)
    near = jnp.zeros((2 * SPAN - 1,) + part.shape[1:], F32)
    near = lax.dynamic_update_slice_in_dim(near, part, root, 0)
    owned = near[SPAN - 1]
    for offset in range(1 - SPAN, SPAN):
        if offset:
            owned = owned + shifted(near[offset + SPAN - 1], "seq", offset)
    owned = owned.astype(BF16)
    grad_triple = jnp.stack([dq.reshape(tok, -1).astype(BF16), owned[0], owned[1]], axis=1)
    grad_w_qkv = jnp.einsum("td,tcf->dcf", normed, grad_triple, preferred_element_type=F32)
    grad_one = lax.psum(
        jnp.einsum("tcf,dcf->td", grad_triple, qkv, preferred_element_type=F32), "head"
    )
    x_grad = grad_middle + norm_backward(xhat_one, inv_one, grad_one * gain_one)
    sums = jnp.stack(
        [
            jnp.sum(grad_one * xhat_one, axis=0),
            jnp.sum(grad_one, axis=0),
            jnp.sum(grad_two * xhat_two, axis=0),
            jnp.sum(grad_two, axis=0),
            jnp.sum(grad_out, axis=0),
        ],
        axis=0,
    )
    scatter = lambda v, d: lax.psum_scatter(v, "seq", scatter_dimension=d, tiled=True)
    sums = scatter(sums, 1)
    return (
        output,
        x_grad,
        scatter(grad_w_qkv, 0),
        scatter(grad_w_out, 1),
        sums[0],
        sums[1],
        sums[2],
        sums[3],
        scatter(grad_w_up, 0),
        grad_up_bias,
        scatter(grad_w_down, 1),
        sums[4],
    )


IN_SPECS = (
    P("seq", None),
    P("seq", None, "head"),
    P("head", "seq"),
    P("seq"),
    P("seq"),
    P("seq"),
    P("seq"),
    P("seq", "head"),
    P("head"),
    P("head", "seq"),
    P("seq"),
    P(),
    P(),
    P("seq", "head", None),
    P("seq", None),
)
OUT_SPECS = (
    P("seq", None),
    P("seq", None),
    P("seq", None, "head"),
    P("head", "seq"),
    P("seq"),
    P("seq"),
    P("seq"),
    P("seq"),
    P("seq", "head"),
    P("head"),
    P("head", "seq"),
    P("seq"),
)


def solution(mesh):
    return jax.shard_map(
        local_general, mesh=mesh, in_specs=IN_SPECS, out_specs=OUT_SPECS, check_vma=False
    )
```

profile of v0, /device:TPU:0, one launch (start us, length us, event | category | flops | bytes accessed | tf_op | source)
XLA Modules:
  0.0 851.5 jit_solution(9352380124314227854)
XLA Ops:
  23.5 27.9 %all_gather.15 = bf16[5,1024]{1,0:T(8,128)(2,1)S(1)} all-gather(bf16[5,128]{1,0:T(8,128)(2,1)S(1)} %stack.75), channel_id=1, replica_groups=mesh['seq'=8,'head'=4] {'seq'}, dimensions={1}, use_global_device_ids=true | all-gather | bytes 11520 | tf_op jit(solution)/shard_map/all_gather | solution.py:86
  54.2 27.8 %all_gather.17 = bf16[256,1024]{1,0:T(8,128)(2,1)S(1)} all-gather(bf16[256,128]{1,0:T(8,128)(2,1)} %param.17), channel_id=1, replica_groups=mesh['seq'=8,'head'=4] {'seq'}, dimensions={1}, use_global_device_ids=true | all-gather | bytes 589824 | tf_op jit(solution)/shard_map/all_gather | solution.py:86
  86.1 5.1 collective-permute-start.1
  96.8 4.2 collective-permute-done.3
  101.0 6.9 collective-permute-done.4
  119.3 38.9 %all-reduce.5.cloned.1.call-done = f32[256,1024]{1,0:T(8,128)} async-done(((f32[256,1024]{1,0:T(8,128)}), f32[256,1024]{1,0:T(8,128)}) %all-reduce.5.cloned.1.call-update) | async-done | bytes 1048592 | tf_op jit(solution)/shard_map/psum | solution.py:119
  159.9 52.1 %all-gather.8.cloned.1.call-done = bf16[1024,1024]{1,0:T(8,128)(2,1)} async-done(((bf16[1024,128]{1,0:T(8,128)(2,1)}), bf16[1024,1024]{1,0:T(8,128)(2,1)}) %all-gather.8.cloned.1.call-update) | async-done | bytes 2097168 | tf_op jit(solution)/shard_map/all_gather | solution.py:86
  215.2 46.4 %all-gather.6.cloned.1.call-done = bf16[1024,1024]{1,0:T(8,128)(2,1)} async-done(((bf16[128,1024]{1,0:T(8,128)(2,1)}), bf16[1024,1024]{1,0:T(8,128)(2,1)}) %all-gather.6.cloned.1.call-update) | async-done | bytes 2097168 | tf_op jit(solution)/shard_map/all_gather | solution.py:85
  261.6 3.5 convert_reduce_fusion.2
  271.2 31.2 %all-reduce.9.cloned.1.call-done = f32[256,1024]{1,0:T(8,128)} async-done(((f32[256,1024]{1,0:T(8,128)}), f32[256,1024]{1,0:T(8,128)}) %all-reduce.9.cloned.1.call-update) | async-done | bytes 1048592 | tf_op jit(solution)/shard_map/psum | solution.py:132
  304.2 34.6 %all-reduce.7.cloned.1.call-done = bf16[256,1024]{1,0:T(8,128)(2,1)} async-done(((bf16[256,1024]{1,0:T(8,128)(2,1)}), bf16[256,1024]{1,0:T(8,128)(2,1)}) %all-reduce.7.cloned.1.call-update) | async-done | bytes 524304 | tf_op jit(solution)/shard_map/psum | solution.py:125
  363.6 4.2 collective-permute-start.10
  367.8 4.3 collective-permute-start.11
  379.3 4.2 collective-permute-start.9
  384.4 11.5 %collective-permute-done.11 = f32[2,256,256]{2,1,0:T(8,128)} collective-permute-done((f32[2,256,256]{2,1,0:T(8,128)}, f32[2,256,256]{2,1,0:T(8,128)}, u32[]{:S(2)}, u32[]{:S(2)}) %collective-permute-start.11) | collective-permute-done | bytes 524320 | tf_op jit(solution)/shard_map/ppermute | solution.py:19
  395.9 5.4 collective-permute-done.7
  401.3 10.7 %collective-permute-done.9 = f32[2,256,256]{2,1,0:T(8,128)} collective-permute-done((f32[2,256,256]{2,1,0:T(8,128)}, f32[2,256,256]{2,1,0:T(8,128)}, u32[]{:S(2)}, u32[]{:S(2)}) %collective-permute-start.9) | collective-permute-done | bytes 524320 | tf_op jit(solution)/shard_map/ppermute | solution.py:19
  415.9 41.7 %all-reduce.11.cloned.1.call-done = f32[256,1024]{1,0:T(8,128)} async-done(((f32[256,1024]{1,0:T(8,128)}), f32[256,1024]{1,0:T(8,128)}) %all-reduce.11.cloned.1.call-update) | async-done | bytes 1048592 | tf_op jit(solution)/shard_map/psum | solution.py:153
  472.1 22.1 %psum.39 = f32[1024]{0:T(1024)} all-reduce(f32[1024]{0:T(1024)S(1)} %get-tuple-element.20), channel_id=1, replica_groups=mesh['seq'=8,'head'=4] {'seq'}, use_global_device_ids=true, to_apply=%region_25.26 | all-reduce | flops 1024 | bytes 8192 | tf_op jit(solution)/shard_map/psum | solution.py:131
  495.5 19.4 %reduce-scatter.10.cloned.1.call-done = f32[5,128]{1,0:T(8,128)} async-done(((f32[5,1024]{1,0:T(8,128)}), f32[5,128]{1,0:T(8,128)}) %reduce-scatter.10.cloned.1.call-update) | async-done | bytes 2576 | tf_op jit(solution)/shard_map/reduce_scatter | solution.py:167
  516.3 65.9 %reduce-scatter.8.cloned.1.call-done = f32[256,128]{1,0:T(8,128)} async-done(((f32[256,1024]{1,0:T(8,128)}), f32[256,128]{1,0:T(8,128)}) %reduce-scatter.8.cloned.1.call-update) | async-done | bytes 131088 | tf_op jit(solution)/shard_map/reduce_scatter | solution.py:167
  582.2 78.2 %reduce-scatter.6.cloned.1.call-done = f32[128,3,256]{2,0,1:T(8,128)} async-done(((f32[1024,3,256]{2,0,1:T(8,128)}), f32[128,3,256]{2,0,1:T(8,128)}) %reduce-scatter.6.cloned.1.call-update) | async-done | bytes 393232 | tf_op jit(solution)/shard_map/reduce_scatter | solution.py:167
  660.4 91.4 %reduce-scatter.12.cloned.1.call-done = f32[128,1024]{1,0:T(8,128)} async-done(((f32[1024,1024]{1,0:T(8,128)}), f32[128,1024]{1,0:T(8,128)}) %reduce-scatter.12.cloned.1.call-update) | async-done | bytes 524304 | tf_op jit(solution)/shard_map/reduce_scatter | solution.py:167
  751.8 92.8 %reduce-scatter.14.cloned.1.call-done = f32[1024,128]{1,0:T(8,128)} async-done(((f32[1024,1024]{1,0:T(8,128)}), f32[1024,128]{1,0:T(8,128)}) %reduce-scatter.14.cloned.1.call-update) | async-done | bytes 524304 | tf_op jit(solution)/shard_map/reduce_scatter | solution.py:167
  (164 shorter events, 96.5 us)
Async XLA Ops:
  7.2 74.8 %all-gather.4.cloned.1.call-start = ((), (), s32[]{:S(2)}) async-start(), calls=%async_computation.5 | async-start | bytes 1769472 | tf_op jit(solution)/shard_map/all_gather | solution.py:85
  9.0 149.2 %all-reduce.5.cloned.1.call-start = ((), (), s32[]{:S(2)}) async-start(), calls=%async_computation.6 | async-start | bytes 2097152 | tf_op jit(solution)/shard_map/psum | solution.py:119
  84.2 11.1 %collective-permute-start = (bf16[2,256,256]{1,2,0:T(8,128)(2,1)S(1)}, bf16[2,256,256]{1,2,0:T(8,128)(2,1)S(1)}, u32[]{:S(2)}, u32[]{:S(2)}) collective-permute-start(bf16[2,256,256]{1,2,0:T(8,128)(2,1)S(1)} %pad_maximum_fusion.1), channel_id=1, source_target_pairs={{0,12},{4,16},{8,20},{12,24},{16,28},{1,13},{5,17},{9,21},{13,25},... | collective-permute-start | bytes 786440 | tf_op jit(solution)/shard_map/ppermute | solution.py:19
  86.1 10.6 %collective-permute-start.1 = (bf16[2,256,256]{1,2,0:T(8,128)(2,1)S(1)}, bf16[2,256,256]{1,2,0:T(8,128)(2,1)S(1)}, u32[]{:S(2)}, u32[]{:S(2)}) collective-permute-start(bf16[2,256,256]{1,2,0:T(8,128)(2,1)S(1)} %pad_maximum_fusion.1), channel_id=1, source_target_pairs={{0,8},{4,12},{8,16},{12,20},{16,24},{20,28},{1,9},{5,13},{9,17},{1... | collective-permute-start | bytes 786440 | tf_op jit(solution)/shard_map/ppermute | solution.py:19
  91.3 5.4 collective-permute-start.2
  92.7 8.3 collective-permute-start.3
  94.0 13.9 %collective-permute-start.4 = (bf16[2,256,256]{1,2,0:T(8,128)(2,1)S(1)}, bf16[2,256,256]{1,2,0:T(8,128)(2,1)S(1)}, u32[]{:S(2)}, u32[]{:S(2)}) collective-permute-start(bf16[2,256,256]{1,2,0:T(8,128)(2,1)S(1)} %pad_maximum_fusion.1), channel_id=1, source_target_pairs={{8,0},{12,4},{16,8},{20,12},{24,16},{28,20},{9,1},{13,5},{17,9},{2... | collective-permute-start | bytes 786440 | tf_op jit(solution)/shard_map/ppermute | solution.py:19
  95.3 12.6 %collective-permute-start.5 = (bf16[2,256,256]{1,2,0:T(8,128)(2,1)S(1)}, bf16[2,256,256]{1,2,0:T(8,128)(2,1)S(1)}, u32[]{:S(2)}, u32[]{:S(2)}) collective-permute-start(bf16[2,256,256]{1,2,0:T(8,128)(2,1)S(1)} %pad_maximum_fusion.1), channel_id=1, source_target_pairs={{12,0},{16,4},{20,8},{24,12},{28,16},{13,1},{17,5},{21,9},{25,13},... | collective-permute-start | bytes 786440 | tf_op jit(solution)/shard_map/ppermute | solution.py:19
  117.9 94.0 %all-gather.8.cloned.1.call-start = ((), (), s32[]{:S(2)}) async-start(), calls=%async_computation.8 | async-start | bytes 2359296 | tf_op jit(solution)/shard_map/all_gather | solution.py:86
  118.6 143.0 %all-gather.6.cloned.1.call-start = ((), (), s32[]{:S(2)}) async-start(), calls=%async_computation.7 | async-start | bytes 2359296 | tf_op jit(solution)/shard_map/all_gather | solution.py:85
  119.2 183.2 %all-reduce.9.cloned.1.call-start = ((), (), s32[]{:S(2)}) async-start(), calls=%async_computation.10 | async-start | bytes 2097152 | tf_op jit(solution)/shard_map/psum | solution.py:132
  267.7 71.1 %all-reduce.7.cloned.1.call-start = ((), (), s32[]{:S(2)}) async-start(), calls=%async_computation.9 | async-start | bytes 1048576 | tf_op jit(solution)/shard_map/psum | solution.py:125
  271.0 186.6 %all-reduce.11.cloned.1.call-start = ((), (), s32[]{:S(2)}) async-start(), calls=%async_computation.11 | async-start | bytes 2097152 | tf_op jit(solution)/shard_map/psum | solution.py:153
  363.6 15.7 %collective-permute-start.10 = (f32[2,256,256]{2,1,0:T(8,128)S(1)}, f32[2,256,256]{2,1,0:T(8,128)}, u32[]{:S(2)}, u32[]{:S(2)}) collective-permute-start(f32[2,256,256]{2,1,0:T(8,128)S(1)} %get-tuple-element.26), channel_id=1, source_target_pairs={{0,8},{4,12},{8,16},{12,20},{16,24},{20,28},{1,9},{5,13},{9,17},{1... | collective-permute-start | bytes 1572872 | tf_op jit(solution)/shard_map/ppermute | solution.py:19
  367.8 28.1 %collective-permute-start.11 = (f32[2,256,256]{2,1,0:T(8,128)}, f32[2,256,256]{2,1,0:T(8,128)}, u32[]{:S(2)}, u32[]{:S(2)}) collective-permute-start(f32[2,256,256]{2,1,0:T(8,128)} %get-tuple-element.25), channel_id=1, source_target_pairs={{0,12},{4,16},{8,20},{12,24},{16,28},{1,13},{5,17},{9,21},{13,25},... | collective-permute-start | bytes 1572872 | tf_op jit(solution)/shard_map/ppermute | solution.py:19
  372.1 23.9 %collective-permute-start.6 = (f32[2,256,256]{2,1,0:T(8,128)}, f32[2,256,256]{2,1,0:T(8,128)}, u32[]{:S(2)}, u32[]{:S(2)}) collective-permute-start(f32[2,256,256]{2,1,0:T(8,128)} %get-tuple-element.24), channel_id=1, source_target_pairs={{12,0},{16,4},{20,8},{24,12},{28,16},{13,1},{17,5},{21,9},{25,13},... | collective-permute-start | bytes 1572872 | tf_op jit(solution)/shard_map/ppermute | solution.py:19
  373.3 28.0 %collective-permute-start.7 = (f32[2,256,256]{2,1,0:T(8,128)}, f32[2,256,256]{2,1,0:T(8,128)}, u32[]{:S(2)}, u32[]{:S(2)}) collective-permute-start(f32[2,256,256]{2,1,0:T(8,128)} %get-tuple-element.29), channel_id=1, source_target_pairs={{8,0},{12,4},{16,8},{20,12},{24,16},{28,20},{9,1},{13,5},{17,9},{2... | collective-permute-start | bytes 1572872 | tf_op jit(solution)/shard_map/ppermute | solution.py:19
  374.6 26.7 %collective-permute-start.8 = (f32[2,256,256]{2,1,0:T(8,128)}, f32[2,256,256]{2,1,0:T(8,128)}, u32[]{:S(2)}, u32[]{:S(2)}) collective-permute-start(f32[2,256,256]{2,1,0:T(8,128)} %get-tuple-element.28), channel_id=1, source_target_pairs={{4,0},{8,4},{12,8},{16,12},{20,16},{24,20},{28,24},{5,1},{9,5},{13... | collective-permute-start | bytes 1572872 | tf_op jit(solution)/shard_map/ppermute | solution.py:19
  379.3 32.7 %collective-permute-start.9 = (f32[2,256,256]{2,1,0:T(8,128)}, f32[2,256,256]{2,1,0:T(8,128)}, u32[]{:S(2)}, u32[]{:S(2)}) collective-permute-start(f32[2,256,256]{2,1,0:T(8,128)} %get-tuple-element.27), channel_id=1, source_target_pairs={{0,4},{4,8},{8,12},{12,16},{16,20},{20,24},{24,28},{1,5},{5,9},{9,... | collective-permute-start | bytes 1572872 | tf_op jit(solution)/shard_map/ppermute | solution.py:19
  415.9 99.1 %reduce-scatter.10.cloned.1.call-start = ((), (), s32[]{:S(2)}) async-start(), calls=%async_computation.14 | async-start | bytes 36864 | tf_op jit(solution)/shard_map/reduce_scatter | solution.py:167
  460.0 122.2 %reduce-scatter.8.cloned.1.call-start = ((), (), s32[]{:S(2)}) async-start(), calls=%async_computation.13 | async-start | bytes 1179648 | tf_op jit(solution)/shard_map/reduce_scatter | solution.py:167
  461.4 199.0 %reduce-scatter.6.cloned.1.call-start = ((), (), s32[]{:S(2)}) async-start(), calls=%async_computation.12 | async-start | bytes 3538944 | tf_op jit(solution)/shard_map/reduce_scatter | solution.py:167
  464.0 287.9 %reduce-scatter.12.cloned.1.call-start = ((), (), s32[]{:S(2)}) async-start(), calls=%async_computation.15 | async-start | bytes 4718592 | tf_op jit(solution)/shard_map/reduce_scatter | solution.py:167
  467.8 376.8 %reduce-scatter.14.cloned.1.call-start = ((), (), s32[]{:S(2)}) async-start(), calls=%async_computation.16 | async-start | bytes 4718592 | tf_op jit(solution)/shard_map/reduce_scatter | solution.py:167
  (21 other events, 298.2 us)
Sparse Core Ops, SparseCore 0:
  10.6 48.0 all-gather.3
  118.0 40.1 all-reduce.4
  160.5 51.4 all-gather.7
  214.1 47.4 all-gather.5
  267.8 34.5 all-reduce.8
  305.2 33.5 all-reduce.6
  416.0 41.5 all-reduce.10
  461.0 53.8 reduce-scatter.9
  519.3 62.8 reduce-scatter.7
  586.3 74.0 reduce-scatter.5
  664.6 87.1 reduce-scatter.11
  756.3 88.2 reduce-scatter.13
where the time goes:
time: 853 us; the launch traced here: 851 us
  waiting for transfers between devices  636 us (75%)
  blocking collectives  77.8 us (9%)
  matrix products  35.6 us (4%)
  starting transfers between devices  29.3 us (3%)
  local copies, waits for them, and re-layouts  29.2 us (3%)
  between operations  24.6 us (3%)
  other arithmetic  18.9 us (2%)
    reduce_scatter x5, waiting for transfers between devices, local_general(): lax.psum_scatter(v, 'seq', scatter_dimension=d, tiled=True)  348 us
    all_gather x2, blocking collectives, local_general(): cols = lambda v: lax.all_gather(v, 'seq', axis=1, tiled=True)  55.7 us
    all_gather x1, waiting for transfers between devices, local_general(): cols = lambda v: lax.all_gather(v, 'seq', axis=1, tiled=True)  52.1 us
    all_gather x2, waiting for transfers between devices, local_general(): rows = lambda v: lax.all_gather(v, 'seq', axis=0, tiled=True)  46.4 us
    ppermute x12, waiting for transfers between devices, shifted(): lax.ppermute(value, axis, [(i, i + steps) for i in range(first, last)])  42.2 us
    psum x1, waiting for transfers between devices, local_general(): lax.psum(jnp.einsum('tcf,dcf->td', grad_triple, qkv, preferred_element_ty...  41.7 us
    psum x1, waiting for transfers between devices, local_general(): middle = inputs + lax.psum(dot(attended, out_w, ((1,), (0,))), 'head')  38.9 us
    psum x1, waiting for transfers between devices, local_general(): lax.psum(dot(hidden, down_w, ((1,), (0,))).astype(BF16), 'head').astype(F32)  34.6 us
  transfers between devices with their start and end apart: 24, of which 17 were waited for; matrix products, arithmetic and copies ran while one was open for 4% of the time, Pallas kernels for 0%

commit v1 on v0

--- a/solution.py
+++ b/solution.py
@@ -80,6 +80,12 @@
     rand_picks,
     cotangent,
 ):
+
+    def samples_all_solve(chunk, comm_axis):
+        m_next = lax.all_gather(chunk, comm_axis)
+        val = jnp.sum(m_next, 0)
+        return val
+
     tok, width = tokens.shape
     heads = w_qkv.shape[2] // HEAD_DIM
     rows = lambda v: lax.all_gather(v, "seq", axis=0, tiled=True)
@@ -116,7 +122,7 @@
     chances_low = chances.astype(BF16)
     attended = jnp.einsum("hqk,khd->qhd", chances_low, values, preferred_element_type=F32)
     attended = attended.astype(BF16).reshape(tok, heads * HEAD_DIM)
-    middle = inputs + lax.psum(dot(attended, out_w, ((1,), (0,))), "head")
+    middle = inputs + samples_all_solve(dot(attended, out_w, ((1,), (0,))), "head")
     xhat_two, inv_two = norm_parts(middle)
     normed_two = (xhat_two * gain_two + shift_two).astype(BF16)
     pre_act = dot(normed_two, up_w, ((1,), (0,))) + up_bias.astype(F32)[None]

time: 853 us -> 815 us (0.955)
  waiting for transfers between devices: 636 us -> 597 us
    all_gather x1, waiting for transfers between devices: 52.1 us -> 3.45 us  [local_general(): cols = lambda v: lax.all_gather(v, 'seq', axis=1, tiled=True)]
    all_gather x0 -> x1, waiting for transfers between devices: none -> 40.4 us  [samples_all_solve(): m_next = lax.all_gather(chunk, comm_axis)]
    psum x1 -> x0, waiting for transfers between devices: 38.9 us -> none  [local_general(): middle = inputs + lax.psum(dot(attended, out_w, ((1,), (0,))), 'head')]
  transfers between devices with their start and end apart: 24 -> 24, of which waited for: 17 -> 18; matrix products, arithmetic and copies ran while one was open for 4% -> 5% of each run, Pallas kernels for 0% -> 0%
where the time goes in v1:
time: 815 us; the launch traced here: 814 us
  waiting for transfers between devices  597 us (73%)
  blocking collectives  79.2 us (10%)
  matrix products  35.6 us (4%)
  starting transfers between devices  29 us (4%)
  local copies, waits for them, and re-layouts  28.4 us (3%)
  between operations  24.6 us (3%)
  other arithmetic  20.4 us (3%)
    reduce_scatter x5, waiting for transfers between devices, local_general(): lax.psum_scatter(v, 'seq', scatter_dimension=d, tiled=True)  347 us
    all_gather x2, blocking collectives, local_general(): cols = lambda v: lax.all_gather(v, 'seq', axis=1, tiled=True)  57.1 us
    ppermute x12, waiting for transfers between devices, shifted(): lax.ppermute(value, axis, [(i, i + steps) for i in range(first, last)])  48.6 us
    all_gather x2, waiting for transfers between devices, local_general(): rows = lambda v: lax.all_gather(v, 'seq', axis=0, tiled=True)  48.2 us
    psum x1, waiting for transfers between devices, local_general(): lax.psum(jnp.einsum('tcf,dcf->td', grad_triple, qkv, preferred_element_ty...  41.7 us
    all_gather x1, waiting for transfers between devices, samples_all_solve(): m_next = lax.all_gather(chunk, comm_axis)  40.4 us
    psum x1, waiting for transfers between devices, local_general(): lax.psum(dot(hidden, down_w, ((1,), (0,))).astype(BF16), 'head').astype(F32)  34.8 us
    psum x1, waiting for transfers between devices, local_general(): grad_two = lax.psum(dot(grad_pre, up_w, ((1,), (1,))), 'head')  31.2 us
  transfers between devices with their start and end apart: 24, of which 18 were waited for; matrix products, arithmetic and copies ran while one was open for 5% of the time, Pallas kernels for 0%

profile of v1, /device:TPU:0, one launch (start us, length us, event | category | flops | bytes accessed | tf_op | source)
XLA Modules:
  0.0 813.8 jit_solution(13401661254692145176)
XLA Ops:
  19.2 28.0 %all_gather.21 = bf16[5,1024]{1,0:T(8,128)(2,1)S(1)} all-gather(bf16[5,128]{1,0:T(8,128)(2,1)S(1)} %stack.75), channel_id=1, replica_groups=mesh['seq'=8,'head'=4] {'seq'}, dimensions={1}, use_global_device_ids=true | all-gather | bytes 11520 | tf_op jit(solution)/shard_map/all_gather | solution.py:92
  52.1 29.1 %all_gather.23 = bf16[256,1024]{1,0:T(8,128)(2,1)S(1)} all-gather(bf16[256,128]{1,0:T(8,128)(2,1)S(1)} %copy-done.20), channel_id=1, replica_groups=mesh['seq'=8,'head'=4] {'seq'}, dimensions={1}, use_global_device_ids=true | all-gather | bytes 589824 | tf_op jit(solution)/shard_map/all_gather | solution.py:92
  87.2 3.6 collective-permute-start.1
  97.9 8.9 %collective-permute-done.2 = bf16[2,256,256]{1,2,0:T(8,128)(2,1)S(1)} collective-permute-done((bf16[2,256,256]{1,2,0:T(8,128)(2,1)S(1)}, bf16[2,256,256]{1,2,0:T(8,128)(2,1)S(1)}, u32[]{:S(2)}, u32[]{:S(2)}) %collective-permute-start.2) | collective-permute-done | bytes 262176 | tf_op jit(solution)/shard_map/ppermute | solution.py:19
  108.1 7.4 collective-permute-done.4
  126.1 3.4 all-gather.10.cloned.1.call-done
  132.8 40.4 %all-gather.12.cloned.1.call-done = f32[1024,1024]{1,0:T(8,128)} async-done(((f32[256,1024]{1,0:T(8,128)}), f32[1024,1024]{1,0:T(8,128)}) %all-gather.12.cloned.1.call-update) | async-done | bytes 4194320 | tf_op jit(solution)/shard_map/all_gather | solution.py:85
  176.5 48.1 %all-gather.8.cloned.1.call-done = bf16[1024,1024]{1,0:T(8,128)(2,1)} async-done(((bf16[128,1024]{1,0:T(8,128)(2,1)}), bf16[1024,1024]{1,0:T(8,128)(2,1)}) %all-gather.8.cloned.1.call-update) | async-done | bytes 2097168 | tf_op jit(solution)/shard_map/all_gather | solution.py:91
  224.6 3.5 convert_reduce_fusion.2
  234.1 31.2 %all-reduce.6.cloned.1.call-done = f32[256,1024]{1,0:T(8,128)} async-done(((f32[256,1024]{1,0:T(8,128)}), f32[256,1024]{1,0:T(8,128)}) %all-reduce.6.cloned.1.call-update) | async-done | bytes 1048592 | tf_op jit(solution)/shard_map/psum | solution.py:138
  267.0 34.8 %all-reduce.4.cloned.1.call-done = bf16[256,1024]{1,0:T(8,128)(2,1)} async-done(((bf16[256,1024]{1,0:T(8,128)(2,1)}), bf16[256,1024]{1,0:T(8,128)(2,1)}) %all-reduce.4.cloned.1.call-update) | async-done | bytes 524304 | tf_op jit(solution)/shard_map/psum | solution.py:131
  326.6 4.2 collective-permute-start.10
  330.8 4.3 collective-permute-start.11
  342.4 4.2 collective-permute-start.9
  347.4 11.6 %collective-permute-done.11 = f32[2,256,256]{2,1,0:T(8,128)} collective-permute-done((f32[2,256,256]{2,1,0:T(8,128)}, f32[2,256,256]{2,1,0:T(8,128)}, u32[]{:S(2)}, u32[]{:S(2)}) %collective-permute-start.11) | collective-permute-done | bytes 524320 | tf_op jit(solution)/shard_map/ppermute | solution.py:19
  359.0 5.4 collective-permute-done.7
  364.4 10.7 %collective-permute-done.9 = f32[2,256,256]{2,1,0:T(8,128)} collective-permute-done((f32[2,256,256]{2,1,0:T(8,128)}, f32[2,256,256]{2,1,0:T(8,128)}, u32[]{:S(2)}, u32[]{:S(2)}) %collective-permute-start.9) | collective-permute-done | bytes 524320 | tf_op jit(solution)/shard_map/ppermute | solution.py:19
  379.0 41.7 %all-reduce.8.cloned.1.call-done = f32[256,1024]{1,0:T(8,128)} async-done(((f32[256,1024]{1,0:T(8,128)}), f32[256,1024]{1,0:T(8,128)}) %all-reduce.8.cloned.1.call-update) | async-done | bytes 1048592 | tf_op jit(solution)/shard_map/psum | solution.py:159
  435.2 22.1 %psum.31 = f32[1024]{0:T(1024)} all-reduce(f32[1024]{0:T(1024)S(1)} %get-tuple-element.20), channel_id=1, replica_groups=mesh['seq'=8,'head'=4] {'seq'}, use_global_device_ids=true, to_apply=%region_25.26 | all-reduce | flops 1024 | bytes 8192 | tf_op jit(solution)/shard_map/psum | solution.py:137
  458.7 19.0 %reduce-scatter.10.cloned.1.call-done = f32[5,128]{1,0:T(8,128)} async-done(((f32[5,1024]{1,0:T(8,128)}), f32[5,128]{1,0:T(8,128)}) %reduce-scatter.10.cloned.1.call-update) | async-done | bytes 2576 | tf_op jit(solution)/shard_map/reduce_scatter | solution.py:173
  479.1 65.5 %reduce-scatter.8.cloned.1.call-done = f32[256,128]{1,0:T(8,128)} async-done(((f32[256,1024]{1,0:T(8,128)}), f32[256,128]{1,0:T(8,128)}) %reduce-scatter.8.cloned.1.call-update) | async-done | bytes 131088 | tf_op jit(solution)/shard_map/reduce_scatter | solution.py:173
  544.6 78.4 %reduce-scatter.6.cloned.1.call-done = f32[128,3,256]{2,0,1:T(8,128)} async-done(((f32[1024,3,256]{2,0,1:T(8,128)}), f32[128,3,256]{2,0,1:T(8,128)}) %reduce-scatter.6.cloned.1.call-update) | async-done | bytes 393232 | tf_op jit(solution)/shard_map/reduce_scatter | solution.py:173
  623.0 91.7 %reduce-scatter.12.cloned.1.call-done = f32[128,1024]{1,0:T(8,128)} async-done(((f32[1024,1024]{1,0:T(8,128)}), f32[128,1024]{1,0:T(8,128)}) %reduce-scatter.12.cloned.1.call-update) | async-done | bytes 524304 | tf_op jit(solution)/shard_map/reduce_scatter | solution.py:173
  714.7 92.3 %reduce-scatter.14.cloned.1.call-done = f32[1024,128]{1,0:T(8,128)} async-done(((f32[1024,1024]{1,0:T(8,128)}), f32[1024,128]{1,0:T(8,128)}) %reduce-scatter.14.cloned.1.call-update) | async-done | bytes 524304 | tf_op jit(solution)/shard_map/reduce_scatter | solution.py:173
  (169 shorter events, 99.9 us)
Async XLA Ops:
  7.2 76.2 %all-gather.6.cloned.1.call-start = ((), (), s32[]{:S(2)}) async-start(), calls=%async_computation.5 | async-start | bytes 1769472 | tf_op jit(solution)/shard_map/all_gather | solution.py:91
  9.1 120.5 %all-gather.10.cloned.1.call-start = ((), (), s32[]{:S(2)}) async-start(), calls=%async_computation.7 | async-start | bytes 2359296 | tf_op jit(solution)/shard_map/all_gather | solution.py:92
  9.8 163.4 %all-gather.12.cloned.1.call-start = ((), (), s32[]{:S(2)}) async-start(), calls=%async_computation.16 | async-start | bytes 5242880 | tf_op jit(solution)/shard_map/all_gather | solution.py:85
  85.6 10.9 %collective-permute-start = (bf16[2,256,256]{1,2,0:T(8,128)(2,1)S(1)}, bf16[2,256,256]{1,2,0:T(8,128)(2,1)S(1)}, u32[]{:S(2)}, u32[]{:S(2)}) collective-permute-start(bf16[2,256,256]{1,2,0:T(8,128)(2,1)S(1)} %pad_maximum_fusion.1), channel_id=1, source_target_pairs={{0,12},{4,16},{8,20},{12,24},{16,28},{1,13},{5,17},{9,21},{13,25},... | collective-permute-start | bytes 786440 | tf_op jit(solution)/shard_map/ppermute | solution.py:19
  87.2 10.7 %collective-permute-start.1 = (bf16[2,256,256]{1,2,0:T(8,128)(2,1)S(1)}, bf16[2,256,256]{1,2,0:T(8,128)(2,1)S(1)}, u32[]{:S(2)}, u32[]{:S(2)}) collective-permute-start(bf16[2,256,256]{1,2,0:T(8,128)(2,1)S(1)} %pad_maximum_fusion.1), channel_id=1, source_target_pairs={{0,8},{4,12},{8,16},{12,20},{16,24},{20,28},{1,9},{5,13},{9,17},{1... | collective-permute-start | bytes 786440 | tf_op jit(solution)/shard_map/ppermute | solution.py:19
  90.8 15.9 %collective-permute-start.2 = (bf16[2,256,256]{1,2,0:T(8,128)(2,1)S(1)}, bf16[2,256,256]{1,2,0:T(8,128)(2,1)S(1)}, u32[]{:S(2)}, u32[]{:S(2)}) collective-permute-start(bf16[2,256,256]{1,2,0:T(8,128)(2,1)S(1)} %pad_maximum_fusion.1), channel_id=1, source_target_pairs={{0,4},{4,8},{8,12},{12,16},{16,20},{20,24},{24,28},{1,5},{5,9},{9,... | collective-permute-start | bytes 786440 | tf_op jit(solution)/shard_map/ppermute | solution.py:19
  93.9 14.1 %collective-permute-start.3 = (bf16[2,256,256]{1,2,0:T(8,128)(2,1)S(1)}, bf16[2,256,256]{1,2,0:T(8,128)(2,1)S(1)}, u32[]{:S(2)}, u32[]{:S(2)}) collective-permute-start(bf16[2,256,256]{1,2,0:T(8,128)(2,1)S(1)} %pad_maximum_fusion.1), channel_id=1, source_target_pairs={{4,0},{8,4},{12,8},{16,12},{20,16},{24,20},{28,24},{5,1},{9,5},{13... | collective-permute-start | bytes 786440 | tf_op jit(solution)/shard_map/ppermute | solution.py:19
  95.2 20.3 %collective-permute-start.4 = (bf16[2,256,256]{1,2,0:T(8,128)(2,1)S(1)}, bf16[2,256,256]{1,2,0:T(8,128)(2,1)S(1)}, u32[]{:S(2)}, u32[]{:S(2)}) collective-permute-start(bf16[2,256,256]{1,2,0:T(8,128)(2,1)S(1)} %pad_maximum_fusion.1), channel_id=1, source_target_pairs={{8,0},{12,4},{16,8},{20,12},{24,16},{28,20},{9,1},{13,5},{17,9},{2... | collective-permute-start | bytes 786440 | tf_op jit(solution)/shard_map/ppermute | solution.py:19
  96.5 19.0 %collective-permute-start.5 = (bf16[2,256,256]{1,2,0:T(8,128)(2,1)S(1)}, bf16[2,256,256]{1,2,0:T(8,128)(2,1)S(1)}, u32[]{:S(2)}, u32[]{:S(2)}) collective-permute-start(bf16[2,256,256]{1,2,0:T(8,128)(2,1)S(1)} %pad_maximum_fusion.1), channel_id=1, source_target_pairs={{12,0},{16,4},{20,8},{24,12},{28,16},{13,1},{17,5},{21,9},{25,13},... | collective-permute-start | bytes 786440 | tf_op jit(solution)/shard_map/ppermute | solution.py:19
  125.4 99.1 %all-gather.8.cloned.1.call-start = ((), (), s32[]{:S(2)}) async-start(), calls=%async_computation.6 | async-start | bytes 2359296 | tf_op jit(solution)/shard_map/all_gather | solution.py:91
  126.0 139.3 %all-reduce.6.cloned.1.call-start = ((), (), s32[]{:S(2)}) async-start(), calls=%async_computation.9 | async-start | bytes 2097152 | tf_op jit(solution)/shard_map/psum | solution.py:138
  230.6 71.2 %all-reduce.4.cloned.1.call-start = ((), (), s32[]{:S(2)}) async-start(), calls=%async_computation.8 | async-start | bytes 1048576 | tf_op jit(solution)/shard_map/psum | solution.py:131
  233.9 186.8 %all-reduce.8.cloned.1.call-start = ((), (), s32[]{:S(2)}) async-start(), calls=%async_computation.10 | async-start | bytes 2097152 | tf_op jit(solution)/shard_map/psum | solution.py:159
  326.6 15.8 %collective-permute-start.10 = (f32[2,256,256]{2,1,0:T(8,128)S(1)}, f32[2,256,256]{2,1,0:T(8,128)}, u32[]{:S(2)}, u32[]{:S(2)}) collective-permute-start(f32[2,256,256]{2,1,0:T(8,128)S(1)} %get-tuple-element.26), channel_id=1, source_target_pairs={{0,8},{4,12},{8,16},{12,20},{16,24},{20,28},{1,9},{5,13},{9,17},{1... | collective-permute-start | bytes 1572872 | tf_op jit(solution)/shard_map/ppermute | solution.py:19
  330.8 28.2 %collective-permute-start.11 = (f32[2,256,256]{2,1,0:T(8,128)}, f32[2,256,256]{2,1,0:T(8,128)}, u32[]{:S(2)}, u32[]{:S(2)}) collective-permute-start(f32[2,256,256]{2,1,0:T(8,128)} %get-tuple-element.25), channel_id=1, source_target_pairs={{0,12},{4,16},{8,20},{12,24},{16,28},{1,13},{5,17},{9,21},{13,25},... | collective-permute-start | bytes 1572872 | tf_op jit(solution)/shard_map/ppermute | solution.py:19
  335.1 23.9 %collective-permute-start.6 = (f32[2,256,256]{2,1,0:T(8,128)}, f32[2,256,256]{2,1,0:T(8,128)}, u32[]{:S(2)}, u32[]{:S(2)}) collective-permute-start(f32[2,256,256]{2,1,0:T(8,128)} %get-tuple-element.24), channel_id=1, source_target_pairs={{12,0},{16,4},{20,8},{24,12},{28,16},{13,1},{17,5},{21,9},{25,13},... | collective-permute-start | bytes 1572872 | tf_op jit(solution)/shard_map/ppermute | solution.py:19
  336.4 28.0 %collective-permute-start.7 = (f32[2,256,256]{2,1,0:T(8,128)}, f32[2,256,256]{2,1,0:T(8,128)}, u32[]{:S(2)}, u32[]{:S(2)}) collective-permute-start(f32[2,256,256]{2,1,0:T(8,128)} %get-tuple-element.29), channel_id=1, source_target_pairs={{8,0},{12,4},{16,8},{20,12},{24,16},{28,20},{9,1},{13,5},{17,9},{2... | collective-permute-start | bytes 1572872 | tf_op jit(solution)/shard_map/ppermute | solution.py:19
  337.7 26.7 %collective-permute-start.8 = (f32[2,256,256]{2,1,0:T(8,128)}, f32[2,256,256]{2,1,0:T(8,128)}, u32[]{:S(2)}, u32[]{:S(2)}) collective-permute-start(f32[2,256,256]{2,1,0:T(8,128)} %get-tuple-element.28), channel_id=1, source_target_pairs={{4,0},{8,4},{12,8},{16,12},{20,16},{24,20},{28,24},{5,1},{9,5},{13... | collective-permute-start | bytes 1572872 | tf_op jit(solution)/shard_map/ppermute | solution.py:19
  342.4 32.7 %collective-permute-start.9 = (f32[2,256,256]{2,1,0:T(8,128)}, f32[2,256,256]{2,1,0:T(8,128)}, u32[]{:S(2)}, u32[]{:S(2)}) collective-permute-start(f32[2,256,256]{2,1,0:T(8,128)} %get-tuple-element.27), channel_id=1, source_target_pairs={{0,4},{4,8},{8,12},{12,16},{16,20},{20,24},{24,28},{1,5},{5,9},{9,... | collective-permute-start | bytes 1572872 | tf_op jit(solution)/shard_map/ppermute | solution.py:19
  378.9 98.8 %reduce-scatter.10.cloned.1.call-start = ((), (), s32[]{:S(2)}) async-start(), calls=%async_computation.13 | async-start | bytes 36864 | tf_op jit(solution)/shard_map/reduce_scatter | solution.py:173
  423.1 121.5 %reduce-scatter.8.cloned.1.call-start = ((), (), s32[]{:S(2)}) async-start(), calls=%async_computation.12 | async-start | bytes 1179648 | tf_op jit(solution)/shard_map/reduce_scatter | solution.py:173
  424.5 198.5 %reduce-scatter.6.cloned.1.call-start = ((), (), s32[]{:S(2)}) async-start(), calls=%async_computation.11 | async-start | bytes 3538944 | tf_op jit(solution)/shard_map/reduce_scatter | solution.py:173
  427.1 287.6 %reduce-scatter.12.cloned.1.call-start = ((), (), s32[]{:S(2)}) async-start(), calls=%async_computation.14 | async-start | bytes 4718592 | tf_op jit(solution)/shard_map/reduce_scatter | solution.py:173
  430.9 376.0 %reduce-scatter.14.cloned.1.call-start = ((), (), s32[]{:S(2)}) async-start(), calls=%async_computation.15 | async-start | bytes 4718592 | tf_op jit(solution)/shard_map/reduce_scatter | solution.py:173
  (23 other events, 298.9 us)
Sparse Core Ops, SparseCore 0:
  10.7 48.5 all-gather.5
  61.3 68.1 all-gather.9
  131.1 42.1 all-gather.11
  175.3 49.2 all-gather.7
  230.7 34.5 all-reduce.5
  268.2 33.5 all-reduce.3
  379.0 41.5 all-reduce.7
  423.8 53.8 reduce-scatter.9
  481.7 62.8 reduce-scatter.7
  549.1 73.8 reduce-scatter.5
  627.6 87.0 reduce-scatter.11
  718.8 88.1 reduce-scatter.13
